TPU v7x, 128 devices: a whole 4x4x4 slice. The times are simulated.
128 devices in a mesh: blk: 64 (over x_lo, y, z, core), grp: 2 (over x_hi).
Axes of the slice: x: 4 (x_hi: 2, x_lo: 2; x = x_hi * 2 + x_lo), y: 4, z: 4, core: 2. Of those that a mesh axis runs over, the one named last changes fastest.
Arguments:
- star_state: float32 [13, 32768], P(None, 'blk')
- active_local: int32 [8192], P(('blk', 'grp')), may hold values from 0 to 511, as said below
- neighbours: int32 [8192, 64], P(('blk', 'grp')), may hold values from 0 to 32767, as said below
- counts: int32 [8192], P(('blk', 'grp')), may hold values from 1 to 64, as said below
Outputs:
- new_state: float32 [6, 8192], P(None, ('blk', 'grp'))
- regular: float32 [6, 8192], P(None, ('blk', 'grp'))
- irregular: float32 [6, 8192], P(None, ('blk', 'grp'))
Inputs may be any that keep to these rules, and one draw needn't show every extreme that they name: `active_local`: distinct within one blk index over its grp devices. Some device's actives all have counts 64. `neighbours`: over one device's live entries (k < counts), each blk index owns (id // 512) at most 64 of them, reached on some device; entries at k >= counts name the active itself.
All inputs are finite; a program needn't handle non-finite values.
Results may differ from a plain program's by a relative error of at most 0.00002.
Values sent between devices are 32-bit elements; how exact they have to be, the bound alone decides.
No kernel may reach another device: no remote copies, remote signals or barrier semaphores. Data moves between devices by JAX's collectives and lax.ppermute only.
A program may use at most 128 MiB of HBM per device.

v0:
```python
import jax
import jax.numpy as jnp
from jax import lax
from jax.sharding import PartitionSpec as P

time_step = 0.0078125
soften_sq = 0.001


def pair_terms(pos_self, vel_self, pos_other, vel_other, mass_other):
    offset_pos = pos_other - pos_self
    rel_vel = vel_other - vel_self
    dist_sq = (
        offset_pos[0] * offset_pos[0]
        + offset_pos[1] * offset_pos[1]
        + offset_pos[2] * offset_pos[2]
        + soften_sq
    )
    inverse = 1.0 / jnp.sqrt(dist_sq)
    strength = mass_other * inverse * inverse * inverse
    radial = (
        offset_pos[0] * rel_vel[0] + offset_pos[1] * rel_vel[1] + offset_pos[2] * rel_vel[2]
    ) / dist_sq
    accel = strength * offset_pos
    jerk_term = strength * (rel_vel - 3.0 * radial * offset_pos)
    return jnp.concatenate([accel, jerk_term], axis=0)


def predict(star_rows):
    position = star_rows[0:3] + time_step * (
        star_rows[3:6] + time_step * (0.5 * star_rows[6:9] + time_step * star_rows[9:12] / 6.0)
    )
    velocity = star_rows[3:6] + time_step * (star_rows[6:9] + 0.5 * time_step * star_rows[9:12])
    return jnp.concatenate([position, velocity, star_rows[12:13]], axis=0)


def correct(own_state, total_sum):
    half_step = 0.5 * time_step
    twelfth = time_step * time_step / 12.0
    new_vel = (
        own_state[3:6]
        + half_step * (own_state[6:9] + total_sum[0:3])
        + twelfth * (own_state[9:12] - total_sum[3:6])
    )
    new_pos = (
        own_state[0:3]
        + half_step * (own_state[3:6] + new_vel)
        + twelfth * (own_state[6:9] - total_sum[0:3])
    )
    return jnp.concatenate([new_pos, new_vel], axis=0)


def regular_part(actives, field_piece):
    pair_vals = pair_terms(
        actives[0:3, :, None],
        actives[3:6, :, None],
        field_piece[0:3, None, :],
        field_piece[3:6, None, :],
        field_piece[6][None, :],
    )
    return jnp.sum(pair_vals, axis=-1)


def per_device(star_state, active_local, neighbours, counts):
    predicted = predict(star_state)
    own_state = jnp.take(star_state, active_local, axis=1)
    actives = jnp.take(predicted, active_local, axis=1)[0:6]
    act_count = active_local.shape[0]
    list_len = neighbours.shape[1]
    field_len = star_state.shape[1]
    star_ids = neighbours.reshape(-1)
    live_mask = jnp.arange(list_len, dtype=jnp.int32)[None, :] < counts[:, None]
    live_flat = live_mask.reshape(-1)
    total_sum = regular_part(actives, lax.all_gather(predicted, "blk", axis=1, tiled=True))
    blk_count = lax.axis_size("blk")
    capacity = (act_count * list_len + blk_count - 1) // blk_count
    total_slots = blk_count * capacity
    owner_blk = star_ids // field_len
    local_index = star_ids % field_len
    owner_table = (
        (owner_blk[:, None] == jnp.arange(blk_count, dtype=jnp.int32)[None, :]) & live_flat[:, None]
    ).astype(jnp.int32)
    rank_in_owner = jnp.sum((jnp.cumsum(owner_table, axis=0) - 1) * owner_table, axis=1)
    slot_index = jnp.where(live_flat, owner_blk * capacity + rank_in_owner, total_slots)
    requests = (
        jnp.zeros((total_slots + 1,), jnp.int32)
        .at[slot_index]
        .set(local_index)[:total_slots]
        .reshape(blk_count, capacity)
    )
    pick_index = jnp.minimum(slot_index, total_slots - 1)
    piece_rows = jnp.take(
        predicted, lax.all_to_all(requests, "blk", split_axis=0, concat_axis=0, tiled=True), axis=1
    )
    fetched = lax.all_to_all(piece_rows, "blk", split_axis=1, concat_axis=1, tiled=True)
    entries = jnp.take(fetched.reshape(7, total_slots), pick_index, axis=1).reshape(
        7, act_count, list_len
    )
    pair_vals = pair_terms(
        actives[0:3, :, None], actives[3:6, :, None], entries[0:3], entries[3:6], entries[6]
    )
    irregular = jnp.sum(jnp.where(live_mask[None], pair_vals, 0.0), axis=-1)
    return (correct(own_state, total_sum), total_sum - irregular, irregular)


def solution(mesh):
    in_specs = (P(None, "blk"), P(("blk", "grp")), P(("blk", "grp"), None), P(("blk", "grp")))
    out_specs = (P(None, ("blk", "grp")), P(None, ("blk", "grp")), P(None, ("blk", "grp")))
    return jax.shard_map(
        per_device, mesh=mesh, in_specs=in_specs, out_specs=out_specs, check_vma=False
    )
```

profile of v0, /device:TPU:1, one launch (start us, length us, event | category | flops | bytes accessed | tf_op | source)
XLA Modules:
  0.0 266.5 jit_solution(11748916779656503969)
XLA Ops:
  0.6 0.0 copy-start
  0.6 0.0 copy-start.2
  0.6 0.7 iota_compare_fusion.2
  1.4 0.8 lt.128
  2.2 0.8 reshape.306
  3.0 0.8 reshape.305
  3.8 0.1 lt.125
  3.9 0.1 lt.133
  4.0 0.8 reshape.308
  4.8 0.1 lt.129
  4.9 0.1 lt.130
  5.0 0.1 lt.127
  5.1 0.1 fusion.10
  5.3 18.4 %reduce-window.6 = s32[64,32,128]{2,1,0:T(8,128)S(1)} reduce-window(s32[64,32,128]{2,1,0:T(8,128)S(1)} %fusion.10, s32[]{:T(128)} %constant.70.clone.1), window={size=1x1x128 pad=0_0x0_0x127_0}, to_apply=%region_1.2 | reduce-window | flops 33292288 | bytes 2097156 | tf_op jit(solution)/shard_map/reduce-window
  23.7 0.3 slice.191
  24.1 0.4 copy.96
  24.5 0.2 reduce-window.9
  24.7 0.3 add_add_fusion.1
  25.1 0.9 fusion.7
  26.0 0.1 compare_select_fusion
  26.1 15.5 %scatter_custom_fusion = s32[4097]{0:T(1024)S(1)} fusion(s32[4096]{0:T(1024)S(1)} %bitcast.62, s32[4096]{0:T(1024)S(1)} %get-tuple-element.32, s32[]{:T(128)} %constant.70.clone.1), kind=kCustom, calls=%fused_computation.80 | custom fusion | bytes 16392 | tf_op jit(solution)/shard_map/scatter | solution.py:88
  41.7 0.7 all_to_all.13
  42.4 10.9 %all-to-all-start = ((s32[64,1,64]{2,1,0:T(1,128)}), s32[64,1,64]{2,1,0:T(1,128)S(1)}, u32[]{:S(2)}, u32[]{:S(2)}) async-start(s32[64,1,64]{2,1,0:T(1,128)} %all_to_all.13), calls=%async_computation | async-start | bytes 65536 | tf_op jit(solution)/shard_map/all_to_all | solution.py:93
  53.3 0.0 copy-done
  53.4 0.0 copy-done.2
  53.4 0.1 copy.84
  53.6 85.3 %all_gather.3 = f32[7,32768]{1,0:T(8,128)S(1)} all-gather(f32[7,512]{1,0:T(8,128)S(1)} %pad_maximum_fusion), channel_id=1, replica_groups=mesh['blk'=64,'grp'=2] {'blk'}, dimensions={1}, use_global_device_ids=true | all-gather | bytes 931840 | tf_op jit(solution)/shard_map/all_gather | solution.py:74
  138.9 0.2 fusion.29
  139.1 0.1 slice.184
  139.3 0.1 copy.82
  139.4 0.6 gather_fusion.1
  140.0 0.1 select_bitcast_fusion.2
  140.1 0.1 fusion.30
  140.2 0.1 copy.85
  140.3 0.1 copy.86
  140.3 0.6 gather_fusion
  141.0 0.1 copy.83
  141.0 16.6 %broadcast_subtract_fusion = (f32[3,64,32768]{2,1,0:T(8,128)}, f32[3,64,32768]{2,1,0:T(8,128)}) fusion(f32[3,64]{1,0:T(4,128)S(1)} %copy.86, f32[3,32768]{1,0:T(4,128)S(1)} %get-tuple-element.23, f32[3,64]{1,0:T(4,128)S(1)} %copy.85, f32[3,32768]{1,0:T(4,128)S(1)} %get-tuple-element.22), kind=kLoop, calls=%fused_computation.8 | loop fusion | flops 12582912 | bytes 51119616 | tf_op jit(solution)/shard_map/sub | solution.py:12
  157.6 20.8 %fusion = (f32[64,32768]{1,0:T(8,128)S(1)}, f32[64,32768]{1,0:T(8,128)}) fusion(f32[3,64,32768]{2,1,0:T(8,128)} %get-tuple-element.35, f32[32768]{0:T(1024)S(1)} %bitcast.55, f32[3,64,32768]{2,1,0:T(8,128)} %get-tuple-element.34), kind=kLoop, calls=%fused_computation.11 | loop fusion | flops 33554432 | bytes 67239936 | tf_op jit(solution)/shard_map/mul | solution.py:24
  178.4 19.7 %subtract_multiply_fusion.1 = (f32[3,64,32768]{2,1,0:T(8,128)}, f32[3,64,32768]{2,1,0:T(8,128)}) fusion(f32[64,32768]{1,0:T(8,128)S(1)} %get-tuple-element.16, f32[3,64]{1,0:T(4,128)S(1)} %copy.85, f32[3,32768]{1,0:T(4,128)S(1)} %get-tuple-element.22, f32[64,32768]{1,0:T(8,128)} %get-tuple-element.17, f32[3,64]{1,0:T(4,128)S(1)} %copy.86, ...), kind=kLoop, calls=%fused_computation.7 | loop fusion | flops 37748736 | bytes 67896832 | tf_op jit(solution)/shard_map/mul | solution.py:24
  198.1 15.9 %maximum_reduce_fusion = f32[6,64]{1,0:T(8,128)S(1)} fusion(f32[3,64,32768]{2,1,0:T(8,128)} %get-tuple-element.19, f32[3,64,32768]{2,1,0:T(8,128)} %get-tuple-element.18), kind=kLoop, calls=%fused_computation.5 | loop fusion | flops 25165440 | bytes 50333184 | tf_op jit(solution)/shard_map/reduce_sum | solution.py:61
  214.0 0.0 all-to-all-done
  214.0 0.1 reshape.328
  214.1 10.8 %gather_fusion.2 = f32[4096,7]{1,0:T(8,128)S(1)} fusion(f32[7,512]{0,1:T(8,128)S(1)} %copy.84, s32[4096]{0:T(1024)S(1)} %broadcast_clamp_fusion.1), kind=kCustom, calls=%fused_computation.2 | custom fusion | bytes 245760 | tf_op jit(solution)/shard_map/jit(_take)/gather | solution.py:92
  224.9 0.7 copy.90
  225.7 0.8 reshape.356
  226.5 4.4 %all-to-all-start.1 = ((f32[64,1,448]{2,1,0:T(1,128)}), f32[64,1,448]{2,1,0:T(1,128)S(1)}, u32[]{:S(2)}, u32[]{:S(2)}) async-start(f32[64,1,448]{2,1,0:T(1,128)} %reshape.356), calls=%async_computation.1 | async-start | bytes 262144 | tf_op jit(solution)/shard_map/all_to_all | solution.py:95
  230.9 0.6 pad_maximum_fusion.1
  231.5 7.8 %all-to-all-done.1 = f32[64,1,448]{2,1,0:T(1,128)S(1)} async-done(((f32[64,1,448]{2,1,0:T(1,128)}), f32[64,1,448]{2,1,0:T(1,128)S(1)}, u32[]{:S(2)}, u32[]{:S(2)}) %all-to-all-start.1) | async-done | bytes 114720 | tf_op jit(solution)/shard_map/all_to_all | solution.py:95
  239.3 0.5 broadcast.376
  239.8 1.0 reduce.2
  240.8 0.1 reshape.357
  240.9 0.7 copy.91
  241.6 14.1 %gather_fusion.3 = f32[4096,7]{1,0:T(8,128)} fusion(f32[7,4096]{0,1:T(8,128)S(1)} %bitcast.51, s32[4096]{0:T(1024)S(1)} %broadcast_clamp_fusion), kind=kCustom, calls=%fused_computation.3 | custom fusion | bytes 245760 | tf_op jit(solution)/shard_map/jit(_take)/gather | solution.py:96
  255.7 3.6 %select_bitcast_fusion = f32[7,4096]{0,1:T(8,128)S(1)} fusion(f32[4096,7]{1,0:T(8,128)} %gather_fusion.3, pred[4096]{0:T(1024)(128)(4,1)S(1)} %compare_and_fusion.1), kind=kLoop, calls=%fused_computation.22 | loop fusion | flops 28672 | bytes 233472 | tf_op jit(solution)/shard_map/jit(_take)/select_n | solution.py:96
  259.3 2.0 fusion.28
  261.4 1.2 slice_reduce_fusion
  262.5 2.3 copy.93
  264.8 0.7 copy.95
  265.5 0.1 squeeze.2
  265.6 0.1 broadcast_subtract_fusion.2
  265.8 0.1 fusion.11
  265.9 0.0 copy-start.1
  265.9 0.6 sub.95
  (23 shorter events, 0.3 us)
Async XLA Ops:
  0.6 52.7 %copy-start = (f32[13,512]{1,0:T(8,128)S(1)}, f32[13,512]{1,0:T(8,128)}, u32[]{:S(2)}) copy-start(f32[13,512]{1,0:T(8,128)} %param.4) | copy-start | bytes 79876
  0.6 52.8 %copy-start.2 = (s32[64]{0:T(128)S(1)}, s32[64]{0:T(128)}, u32[]{:S(2)}) copy-start(s32[64]{0:T(128)} %param.5) | copy-start | bytes 772
  42.4 171.6 %all-to-all-start = ((s32[64,1,64]{2,1,0:T(1,128)}), s32[64,1,64]{2,1,0:T(1,128)S(1)}, u32[]{:S(2)}, u32[]{:S(2)}) async-start(s32[64,1,64]{2,1,0:T(1,128)} %all_to_all.13), calls=%async_computation | async-start | bytes 65536 | tf_op jit(solution)/shard_map/all_to_all | solution.py:93
  226.5 12.8 %all-to-all-start.1 = ((f32[64,1,448]{2,1,0:T(1,128)}), f32[64,1,448]{2,1,0:T(1,128)S(1)}, u32[]{:S(2)}, u32[]{:S(2)}) async-start(f32[64,1,448]{2,1,0:T(1,128)} %reshape.356), calls=%async_computation.1 | async-start | bytes 262144 | tf_op jit(solution)/shard_map/all_to_all | solution.py:95
  265.9 0.6 copy-start.1
where the time goes:
time: 267 us
  other arithmetic  100 us (37%)
  blocking collectives  85.3 us (32%)
  local copies, waits for them, and re-layouts  56.9 us (21%)
  starting transfers between devices  15.3 us (6%)
  waiting for transfers between devices  7.83 us (3%)
    all_gather x1, blocking collectives, per_device(): lax.all_gather(predicted, 'blk', axis=1, tiled=True)  85.3 us
    mul x4, other arithmetic, pair_terms(): accel = strength * offset_pos  40.5 us
    another operation x2, other arithmetic  18.6 us
    sub x2, other arithmetic, pair_terms(): rel_vel = vel_other - vel_self  16.7 us
    reduce_sum x1, other arithmetic, regular_part(): return jnp.sum(pair_vals, axis=-1)  15.9 us
    scatter x1, local copies, waits for them, and re-layouts, per_device(): requests = jnp.zeros((total_slots + 1,), jnp.int32).at[slot_index].set(lo...  15.5 us
    gather x1, local copies, waits for them, and re-layouts, per_device(): jnp.take(fetched.reshape(7, total_slots), pick_index, axis=1)  14.1 us
    gather x2, local copies, waits for them, and re-layouts, per_device(): jnp.take(predicted, lax.all_to_all(requests, 'blk', split_axis=0, concat_...  11.5 us
  transfers between devices with their start and end apart: 2, of which 1 were waited for; matrix products, arithmetic and copies ran while one was open for 28% of the time, Pallas kernels for 0%

commit v1 on v0

v1 whole, which is shorter than its diff:
```python
import jax
import jax.numpy as jnp
from jax import lax
from jax.experimental import pallas as pl
from jax.experimental.pallas import tpu as pltpu
from jax.sharding import Mesh, PartitionSpec as P

time_step = 0.0078125
soften_sq = 0.001

LANES = 128
ROWS = 4
CHUNK = 7 * ROWS
ACT = 64
HALF = ACT // 2
FAR = ("xl", "y", "z")


def column(row):
    on_diag = lax.broadcasted_iota(jnp.int32, (ACT, ACT), 0) == lax.broadcasted_iota(
        jnp.int32, (ACT, ACT), 1
    )
    spread = jnp.where(on_diag, jnp.broadcast_to(row, (ACT, ACT)).astype(jnp.float32), 0.0)
    return jnp.sum(spread, axis=1, keepdims=True).astype(jnp.int32)


def prep_kernel(copies, state_ref, local_ref, chunk_ref, own_ref):
    state = [state_ref[i : i + 1, :] for i in range(13)]
    predicted = []
    for i in range(3):
        predicted.append(
            state[i]
            + time_step
            * (
                state[3 + i]
                + time_step * (0.5 * state[6 + i] + time_step * state[9 + i] / 6.0)
            )
        )
    for i in range(3):
        predicted.append(state[3 + i] + time_step * (state[6 + i] + 0.5 * time_step * state[9 + i]))
    predicted.append(state[12])
    pieces = []
    for value in predicted:
        for q in range(ROWS):
            pieces.append(value[:, q * LANES : (q + 1) * LANES])
    chunk = jnp.concatenate(pieces, axis=0)
    for s in range(copies):
        chunk_ref[s] = chunk
    local = column(local_ref[...])
    lane = lax.broadcasted_iota(jnp.int32, (ACT, LANES), 1)
    picks = [jnp.broadcast_to(local, (ACT, LANES)) == lane + q * LANES for q in range(ROWS)]
    for i, value in enumerate(state[:12] + predicted[:6]):
        total = jnp.zeros((ACT, LANES), jnp.float32)
        for q in range(ROWS):
            row = jnp.broadcast_to(value[:, q * LANES : (q + 1) * LANES], (ACT, LANES))
            total = jnp.where(picks[q], row, total)
        own_ref[i] = jnp.broadcast_to(jnp.sum(total, axis=1, keepdims=True), (ACT, LANES))


def pair_terms(active, star):
    dx = [star[i] - active[i] for i in range(3)]
    dv = [star[3 + i] - active[3 + i] for i in range(3)]
    dist_sq = dx[0] * dx[0] + dx[1] * dx[1] + (dx[2] * dx[2] + soften_sq)
    inv = lax.rsqrt(dist_sq)
    inv_sq = inv * inv
    strength = (star[6] * inv) * inv_sq
    radial = (dx[0] * dv[0] + dx[1] * dv[1] + dx[2] * dv[2]) * inv_sq
    push = (3.0 * strength) * radial
    return [strength * d for d in dx] + [strength * dv[i] - push * dx[i] for i in range(3)]


def field_pass(parity, stars_ref, own_ref, near_ref, sums, rows):
    shards = stars_ref.shape[0]
    for part in range(4):
        active = [
            [own_ref[12 + i, (2 * part + g) * 8 : (2 * part + g + 1) * 8, :] for i in range(6)]
            for g in range(2)
        ]
        ids = near_ref[part * 8 : (part + 1) * 8, :]
        row_id = (ids >> 7) - parity * ROWS
        lane_id = ids & (LANES - 1)

        def step(s, carry):
            acc, found = carry
            acc = [list(a) for a in acc]
            found = list(found)
            for q in range(ROWS):
                star = [
                    jnp.broadcast_to(stars_ref[s, pl.ds(v * ROWS + q, 1), :], (8, LANES))
                    for v in range(7)
                ]
                hit = row_id == s * (2 * ROWS) + q
                for v in range(7):
                    value = jnp.take_along_axis(
                        star[v], lane_id, axis=1, mode="promise_in_bounds"
                    )
                    found[v] = jnp.where(hit, value, found[v])
                for g in range(2):
                    terms = pair_terms(active[g], star)
                    acc[g] = [a + t for a, t in zip(acc[g], terms)]
            return (tuple(tuple(a) for a in acc), tuple(found))

        init = (
            tuple(tuple(sums[i, 2 * part + g] for i in range(6)) for g in range(2)),
            tuple(rows[v, part] for v in range(7)),
        )
        yield part, lax.fori_loop(0, shards, step, init)


class Zero:
    def __getitem__(self, index):
        return jnp.zeros((8, LANES), jnp.float32)


class Tiles:
    def __init__(self, ref):
        self.ref = ref

    def __getitem__(self, index):
        first, tile = index
        return self.ref[first, tile * 8 : (tile + 1) * 8, :]


def first_kernel(core_ref, stars_ref, own_ref, near_ref, sum_ref, row_ref):
    parity = core_ref[0]
    for part, (acc, found) in field_pass(parity, stars_ref, own_ref, near_ref, Zero(), Zero()):
        for g in range(2):
            for i in range(6):
                sum_ref[i, (2 * part + g) * 8 : (2 * part + g + 1) * 8, :] = acc[g][i]
        for v in range(7):
            row_ref[v, part * 8 : (part + 1) * 8, :] = found[v]


def second_kernel(
    core_ref,
    stars_ref,
    own_ref,
    near_ref,
    sum_ref,
    row_ref,
    count_ref,
    new_ref,
    regular_ref,
    irregular_ref,
    total_sc,
    entry_sc,
):
    parity = 1 - core_ref[0]
    for part, (acc, found) in field_pass(
        parity, stars_ref, own_ref, near_ref, Tiles(sum_ref), Tiles(row_ref)
    ):
        for g in range(2):
            for i in range(6):
                total_sc[i, (2 * part + g) * 8 : (2 * part + g + 1) * 8, :] = acc[g][i]
        for v in range(7):
            entry_sc[v, part * 8 : (part + 1) * 8, :] = found[v]

    lane = lax.broadcasted_iota(jnp.int32, (HALF, LANES), 1)
    low = lane < HALF * 2
    count = column(count_ref[...])
    count = jnp.where(low, count[:HALF], count[HALF:])
    live = (lane & (ACT - 1)) < count
    active = [
        jnp.where(low, own_ref[12 + i, 0:HALF, :], own_ref[12 + i, HALF:ACT, :]) for i in range(6)
    ]
    terms = pair_terms(active, [entry_sc[v] for v in range(7)])
    irregular = []
    for term in terms:
        both = [
            jnp.sum(jnp.where(live & side, term, 0.0), axis=1, keepdims=True)
            for side in (low, jnp.logical_not(low))
        ]
        irregular.append(jnp.concatenate(both, axis=0))
    total = [jnp.sum(total_sc[i], axis=1, keepdims=True) for i in range(6)]
    own = [own_ref[i][:, 0:1] for i in range(12)]
    half_step = 0.5 * time_step
    twelfth = time_step * time_step / 12.0
    new_vel = [
        own[3 + i] + half_step * (own[6 + i] + total[i]) + twelfth * (own[9 + i] - total[3 + i])
        for i in range(3)
    ]
    new_pos = [
        own[i] + half_step * (own[3 + i] + new_vel[i]) + twelfth * (own[6 + i] - total[i])
        for i in range(3)
    ]
    regular = [total[i] - irregular[i] for i in range(6)]
    table = jnp.zeros((LANES, LANES), jnp.float32)
    column_id = lax.broadcasted_iota(jnp.int32, (ACT, LANES), 1)
    table = jnp.zeros((ACT, LANES), jnp.float32)
    for at, values in ((0, new_pos + new_vel), (8, regular), (16, irregular)):
        for i, value in enumerate(values):
            table = jnp.where(column_id == at + i, value, table)
    turned = jnp.concatenate([table, table], axis=0).T
    new_ref[...] = turned[0:6, 0:ACT]
    regular_ref[...] = turned[8:14, 0:ACT]
    irregular_ref[...] = turned[16:22, 0:ACT]


VM = pl.BlockSpec(memory_space=pltpu.VMEM)
SM = pl.BlockSpec(memory_space=pltpu.SMEM)


def shape(*dims):
    return jax.ShapeDtypeStruct(dims, jnp.float32)


def per_device(star_state, active_local, neighbours, counts):
    copies = lax.axis_size(FAR)
    chunks, own = pl.pallas_call(
        lambda *refs: prep_kernel(copies, *refs),
        out_shape=(shape(copies, CHUNK, LANES), shape(18, ACT, LANES)),
        in_specs=[VM, VM],
        out_specs=(VM, VM),
        name="prep",
    )(star_state, active_local.reshape(1, ACT))
    near = jnp.concatenate([neighbours[:HALF], neighbours[HALF:]], axis=1)
    core = lax.axis_index("c").astype(jnp.int32).reshape(1)
    mine = lax.all_to_all(chunks, FAR, 0, 0, tiled=True)
    other = lax.ppermute(mine, "c", [(0, 1), (1, 0)])
    stars = copies * ROWS * LANES
    cost = pl.CostEstimate(flops=45 * ACT * stars, bytes_accessed=28 * stars, transcendentals=0)
    sums, rows = pl.pallas_call(
        first_kernel,
        out_shape=(shape(6, ACT, LANES), shape(7, HALF, LANES)),
        in_specs=[SM, VM, VM, VM],
        out_specs=(VM, VM),
        cost_estimate=cost,
        name="first_half",
    )(core, mine, own, near)
    return pl.pallas_call(
        second_kernel,
        out_shape=(shape(6, ACT), shape(6, ACT), shape(6, ACT)),
        in_specs=[SM] + [VM] * 6,
        out_specs=(VM, VM, VM),
        scratch_shapes=[
            pltpu.VMEM((6, ACT, LANES), jnp.float32),
            pltpu.VMEM((7, HALF, LANES), jnp.float32),
        ],
        cost_estimate=cost,
        name="second_half",
    )(core, other, own, near, sums, rows, counts.reshape(1, ACT))


def solution(mesh):
    fine = Mesh(mesh.devices.reshape(2, 4, 4, 2, 2), ("xl", "y", "z", "c", "g"))
    blk = ("xl", "y", "z", "c")
    every = blk + ("g",)
    in_specs = (P(None, blk), P(every), P(every, None), P(every))
    out_specs = (P(None, every),) * 3
    return jax.shard_map(
        per_device, mesh=fine, in_specs=in_specs, out_specs=out_specs, check_vma=False
    )
```

time: 267 us -> 57.4 us (0.21)
  other arithmetic: 100 us -> 0.68 us
  blocking collectives: 85.3 us -> 19.9 us
  local copies, waits for them, and re-layouts: 56.9 us -> 0.79 us
  Pallas kernels: 0 us -> 32.5 us
  starting transfers between devices: 15.3 us -> 2.47 us
  waiting for transfers between devices: 7.83 us -> 0.01 us
    all_gather x1 -> x0, blocking collectives: 85.3 us -> none  [per_device(): lax.all_gather(predicted, 'blk', axis=1, tiled=True)]
    mul x4 -> x0, other arithmetic: 40.5 us -> none  [pair_terms(): accel = strength * offset_pos]
    pallas_call x0 -> x3, Pallas kernels: none -> 32.5 us  [the longest x1 15.5 us: per_device(): pl.pallas_call(second_kernel, out_shape=(shape(6, ACT), shape(6, ACT), sh...]
    gather x6 -> x0, local copies, waits for them, and re-layouts: 26.8 us -> none  [the longest x1 14.1 us: per_device(): jnp.take(fetched.reshape(7, total_slots), pick_index, axis=1)]
    all_to_all x0 -> x1, blocking collectives: none -> 19.9 us  [per_device(): mine = lax.all_to_all(chunks, FAR, 0, 0, tiled=True)]
    another operation x2 -> x0, other arithmetic: 18.6 us -> none
    sub x4 -> x0, other arithmetic: 17.7 us -> none  [the longest x2 16.7 us: pair_terms(): rel_vel = vel_other - vel_self]
    reduce_sum x3 -> x0, other arithmetic: 16.9 us -> none  [the longest x1 15.9 us: regular_part(): return jnp.sum(pair_vals, axis=-1)]
  transfers between devices with their start and end apart: 2 -> 1, of which waited for: 1 -> 0; matrix products, arithmetic and copies ran while one was open for 28% -> 1% of each run, Pallas kernels for 0% -> 26%
where the time goes in v1:
time: 57.4 us; the launch traced here: 57 us
  Pallas kernels  32.5 us (57%)
  blocking collectives  19.9 us (35%)
  starting transfers between devices  2.47 us (4%)
  local copies, waits for them, and re-layouts  0.79 us (1%)
  other arithmetic  0.68 us (1%)
  between operations  0.64 us (1%)
    all_to_all x1, blocking collectives, per_device(): mine = lax.all_to_all(chunks, FAR, 0, 0, tiled=True)  19.9 us
    pallas_call x1, Pallas kernels, per_device(): pl.pallas_call(second_kernel, out_shape=(shape(6, ACT), shape(6, ACT), sh...  15.5 us
    pallas_call x1, Pallas kernels, per_device(): pl.pallas_call(first_kernel, out_shape=(shape(6, ACT, LANES), shape(7, HA...  15 us
    ppermute x1, starting transfers between devices, per_device(): other = lax.ppermute(mine, 'c', [(0, 1), (1, 0)])  2.47 us
    pallas_call x1, Pallas kernels, per_device(): pl.pallas_call(lambda *refs: prep_kernel(copies, *refs), out_shape=(shape...  2.02 us
  transfers between devices with their start and end apart: 1, of which 0 were waited for; matrix products, arithmetic and copies ran while one was open for 1% of the time, Pallas kernels for 26%

profile of v1, /device:TPU:1, one launch (start us, length us, event | category | flops | bytes accessed | tf_op | source)
XLA Modules:
  0.0 57.0 jit_solution(9448161830881437371)
XLA Ops:
  0.6 2.0 %prep.1 = (f32[32,28,128]{2,1,0:T(8,128)}, f32[18,64,128]{2,1,0:T(8,128)}) custom-call(f32[13,512]{1,0:T(8,128)} %refs_0_.1, s32[1,64]{1,0:T(1,128)} %bitcast.4), custom_call_target="tpu_custom_call" | custom-call | tf_op jit(solution)/shard_map/prep/pallas_call | solution.py:209
  2.6 0.0 copy-start.2
  2.6 19.9 %all_to_all.5.stars_ref = f32[32,28,128]{2,1,0:T(8,128)S(1)} all-to-all(f32[32,28,128]{2,1,0:T(8,128)} %get-tuple-element.7), channel_id=1, replica_groups=mesh['xl'=2,'y'=4,'z'=4,'c'=2,'g'=2] {'xl','y','z'}, dimensions={0} | all-to-all | bytes 917504 | tf_op jit(solution)/shard_map/all_to_all | solution.py:218
  22.6 0.0 copy-start
  22.6 2.5 %collective-permute-start = (f32[32,28,128]{2,1,0:T(8,128)S(1)}, f32[32,28,128]{2,1,0:T(8,128)S(1)}, u32[]{:S(2)}, u32[]{:S(2)}) collective-permute-start(f32[32,28,128]{2,1,0:T(8,128)S(1)} %all_to_all.5.stars_ref), channel_id=1, source_target_pairs={{0,2},{2,0},{1,3},{3,1},{4,6},{6,4},{5,7},{7,5},{8,10},{10,8},{9,1... | collective-permute-start | bytes 1376264 | tf_op jit(solution)/shard_map/ppermute | solution.py:219
  25.0 0.0 copy-done.2
  25.0 0.7 %pad_add_fusion.near_ref = s32[32,128]{1,0:T(8,128)} fusion(s32[32,64]{1,0:T(8,128)S(1)} %get-tuple-element.12, s32[32,64]{1,0:T(8,128)S(1)} %get-tuple-element.11), kind=kLoop, calls=%fused_computation | loop fusion | flops 4096 | bytes 32768 | tf_op jit(solution)/shard_map/concatenate | solution.py:216
  25.7 0.0 copy-done
  25.7 15.0 %first_half.1 = (f32[6,64,128]{2,1,0:T(8,128)}, f32[7,32,128]{2,1,0:T(8,128)}) custom-call(s32[1]{0:T(128)} %bitcast.core_ref, f32[32,28,128]{2,1,0:T(8,128)} %copy-done, f32[18,64,128]{2,1,0:T(8,128)} %get-tuple-element.8.own_ref, s32[32,128]{1,0:T(8,128)} %pad_add_fusion.near_ref), custom_call_target="tpu_custom_call" | custom-call | flops 47185920 | bytes 458752 | tf_op jit(solution)/shard_map/first_half/pallas_call | solution.py:222
  40.7 0.0 collective-permute-done.stars_ref
  40.7 0.0 copy-start.1
  40.7 0.8 %copy-done.1 = f32[32,28,128]{2,1,0:T(8,128)} copy-done((f32[32,28,128]{2,1,0:T(8,128)}, f32[32,28,128]{2,1,0:T(8,128)S(1)}, u32[]{:S(2)}) %copy-start.1) | copy-done | bytes 458776
  41.5 15.5 %second_half.1 = (f32[6,64]{1,0:T(8,128)}, f32[6,64]{1,0:T(8,128)}, f32[6,64]{1,0:T(8,128)}) custom-call(s32[1]{0:T(128)} %bitcast.core_ref, f32[32,28,128]{2,1,0:T(8,128)} %copy-done.1, f32[18,64,128]{2,1,0:T(8,128)} %get-tuple-element.8.own_ref, s32[32,128]{1,0:T(8,128)} %pad_add_fusion.near_ref, f32[6,64,128]{2,1,0:T(8,128)} %get-tuple-element.9.sum_ref, ...), custom_call_target="tpu_custom_call" | custom-call | flops 47185920 | bytes 458752 | tf_op jit(solution)/shard_map/second_half/pallas_call | solution.py:230
  (1 shorter events, 0.0 us)
Async XLA Ops:
  2.6 22.4 %copy-start.2 = (s32[64,64]{1,0:T(8,128)S(1)}, s32[64,64]{1,0:T(8,128)}, u32[]{:S(2)}) copy-start(s32[64,64]{1,0:T(8,128)} %param.6) | copy-start | bytes 49156
  22.6 3.2 %copy-start = (f32[32,28,128]{2,1,0:T(8,128)}, f32[32,28,128]{2,1,0:T(8,128)S(1)}, u32[]{:S(2)}) copy-start(f32[32,28,128]{2,1,0:T(8,128)S(1)} %all_to_all.5.stars_ref) | copy-start | bytes 1376260
  22.6 18.1 %collective-permute-start = (f32[32,28,128]{2,1,0:T(8,128)S(1)}, f32[32,28,128]{2,1,0:T(8,128)S(1)}, u32[]{:S(2)}, u32[]{:S(2)}) collective-permute-start(f32[32,28,128]{2,1,0:T(8,128)S(1)} %all_to_all.5.stars_ref), channel_id=1, source_target_pairs={{0,2},{2,0},{1,3},{3,1},{4,6},{6,4},{5,7},{7,5},{8,10},{10,8},{9,1... | collective-permute-start | bytes 1376264 | tf_op jit(solution)/shard_map/ppermute | solution.py:219
  40.7 0.8 %copy-start.1 = (f32[32,28,128]{2,1,0:T(8,128)}, f32[32,28,128]{2,1,0:T(8,128)S(1)}, u32[]{:S(2)}) copy-start(f32[32,28,128]{2,1,0:T(8,128)S(1)} %collective-permute-done.stars_ref) | copy-start | bytes 1376260
